TPU v7x, 32 devices: a whole 2x2x4 slice. The times are simulated.
32 devices in a mesh: egrp: 2 (over x), space: 16 (over z, y, core).
Axes of the slice: x: 2, y: 2, z: 4, core: 2. Of those that a mesh axis runs over, the one named last changes fastest.
Arguments:
- dist: float32 [2, 1024, 64, 128], P(None, 'egrp', 'space'), may hold values from -12 to 12
- hist_x: bfloat16 [4, 2, 1024, 64, 128], P(None, None, 'egrp', 'space'), may hold values from -6 to 6
- hist_g: bfloat16 [4, 2, 1024, 64, 128], P(None, None, 'egrp', 'space'), may hold values from -12 to 12
- mobility: float32 [64, 128], P('space'), may hold values from 0.2 to 2
- region: int32 [64, 128], P('space'), may hold values from 0 to 3
- phonon_bins: int32 [4], replicated, may hold values from 48 to 64, as said below
- coupling: float32 [4], replicated, may hold values from 0.2 to 1.5
- hist_used: int32 [2, 4], replicated, may hold values 0 or 1
Outputs:
- drifted: float32 [2, 1024, 64, 128], P(None, 'egrp', 'space')
Inputs may be any that keep to these rules, and one draw needn't show every extreme that they name: `phonon_bins`: each value lies in 48 to 64; both ends occur.
All inputs are finite; a program needn't handle non-finite values.
Results may differ from a plain program's by a relative error of at most 0.0003.
Values sent between devices are 32-bit elements; how exact they have to be, the bound alone decides.
A program may use at most 128 MiB of HBM per device.

v0:
```python
import jax
import jax.numpy as jnp
from jax import lax
from jax.sharding import PartitionSpec as P

NE = 1024
HISTORY = 4
NREGION = 4
KMAX = 64
COLS = 64


def extended(block, sides, width):
    for axis, dim in sides:
        count = lax.axis_size(axis)
        forward = [(i, i + 1) for i in range(count - 1)]
        backward = [(target, source) for source, target in forward]
        low = lax.ppermute(
            lax.slice_in_dim(block, block.shape[dim] - width, None, axis=dim), axis, forward
        )
        high = lax.ppermute(lax.slice_in_dim(block, 0, width, axis=dim), axis, backward)
        block = jnp.concatenate([low, block, high], axis=dim)
    return block


def add_face(total, field, moved, mobility, moved_mob, valid):
    return total + jnp.where(valid, 0.5 * (mobility + moved_mob) * (moved - field), 0.0)


def local(dist, hist_x, hist_g, mobility, region, phonon_bins, coupling, hist_used):
    width = dist.shape[1]
    rows = dist.shape[2]
    cells = dist.shape[3]
    flat_g = hist_g.reshape(HISTORY, 2, -1)
    energy_ids = lax.axis_index("egrp") * width + jnp.arange(width, dtype=jnp.int32)
    dos = jnp.sqrt((energy_ids.astype(jnp.float32) + 0.5) / NE)
    even = dist[0]
    odd = dist[1]
    outrate = jnp.zeros(even.shape, jnp.float32)
    lam = jnp.zeros(region.shape, jnp.float32)
    for index in range(NREGION):
        offset = phonon_bins[index]
        lower = energy_ids - offset
        upper = energy_ids + offset
        dos_low = jnp.where(
            lower >= 0, jnp.sqrt((jnp.maximum(lower, 0).astype(jnp.float32) + 0.5) / NE), 0.0
        )
        dos_high = jnp.where(upper < NE, jnp.sqrt((upper.astype(jnp.float32) + 0.5) / NE), 0.0)
        rate = coupling[index] * (1.5 * dos_low + 0.5 * dos_high)
        outrate = jnp.where((region == index)[None], rate[:, None, None], outrate)
        lam = jnp.where(region == index, coupling[index], lam)
    column = lax.all_to_all(
        even.reshape(width, rows * cells), "egrp", split_axis=1, concat_axis=0, tiled=True
    )
    span = column.shape[1]
    column_region = lax.dynamic_slice_in_dim(
        region.reshape(-1), lax.axis_index("egrp") * span, span
    )
    padded = jnp.pad(column, ((KMAX, KMAX), (0, 0)))
    total = column.shape[0]
    partial_sum = jnp.zeros(column.shape, jnp.float32)
    for index in range(NREGION):
        offset = phonon_bins[index]
        above = lax.dynamic_slice_in_dim(padded, KMAX + offset, total, 0)
        below = lax.dynamic_slice_in_dim(padded, KMAX - offset, total, 0)
        partial_sum = jnp.where(
            (column_region == index)[None], 1.5 * above + 0.5 * below, partial_sum
        )
    shifted = lax.all_to_all(partial_sum, "egrp", split_axis=0, concat_axis=1, tiled=True).reshape(
        width, rows, cells
    )
    gain_in = lam[None] * dos[:, None, None] * shifted
    new_even = (even + gain_in) / (1.0 + outrate)
    new_odd = odd / (1.0 + outrate + lam[None])
    res = jnp.stack([new_even - even, new_odd - odd])
    res_flat = res.reshape(2, -1)
    cross = jnp.transpose(jnp.sum(flat_g.astype(jnp.float32) * res_flat[None], axis=2))
    self_term = jnp.sum(res_flat * res_flat, axis=1)
    among = lax.dot_general(
        flat_g, flat_g, (((2,), (2,)), ((1,), (1,))), preferred_element_type=jnp.float32
    )
    among, cross, self_term = lax.psum((among, cross, self_term), ("egrp", "space"))
    fields = []
    for field in range(2):
        top = jnp.concatenate([self_term[field][None], cross[field]])[None, :]
        lower_rows = jnp.concatenate([cross[field][:, None], among[field]], axis=1)
        gram = jnp.concatenate([top, lower_rows], axis=0)
        valid = jnp.concatenate([jnp.ones((1,), jnp.float32), hist_used[field].astype(jnp.float32)])
        masked = valid[:, None] * valid[None, :] * gram + jnp.diag(1.0 - valid) * gram[0, 0]
        factor = jnp.linalg.cholesky(masked)
        weights = jax.scipy.linalg.cho_solve((factor, True), valid)
        coeffs = weights / jnp.sum(weights)
        part_mix = coeffs[0] * (dist[field] + 0.5 * res[field])
        for index in range(HISTORY):
            part_mix = part_mix + coeffs[index + 1] * (
                hist_x[index, field].astype(jnp.float32)
                + 0.5 * hist_g[index, field].astype(jnp.float32)
            )
        fields.append(part_mix)
    mixed = jnp.stack(fields)
    mob_block = mobility[None, None]
    wide_field, wide_mob = (
        extended(mixed, (("space", 2),), 1),
        extended(mob_block, (("space", 2),), 1),
    )
    row_ids = lax.axis_index("space") * rows + jnp.arange(rows, dtype=jnp.int32)
    all_rows = lax.axis_size("space") * rows
    cell_ids = jnp.arange(cells, dtype=jnp.int32)
    column_ids = cell_ids % COLS
    lap = jnp.zeros(mixed.shape, jnp.float32)
    lap = add_face(
        lap,
        mixed,
        wide_field[:, :, 0:rows],
        mob_block,
        wide_mob[:, :, 0:rows],
        (row_ids > 0)[:, None],
    )
    lap = add_face(
        lap,
        mixed,
        wide_field[:, :, 2 : rows + 2],
        mob_block,
        wide_mob[:, :, 2 : rows + 2],
        (row_ids < all_rows - 1)[:, None],
    )
    for shift_by, valid_cells in (
        (1, column_ids > 0),
        (-1, column_ids < COLS - 1),
        (COLS, cell_ids >= COLS),
        (-COLS, cell_ids < COLS),
    ):
        moved = jnp.roll(mixed, shift_by, axis=3)
        moved_mob = jnp.roll(mob_block, shift_by, axis=3)
        lap = add_face(lap, mixed, moved, mob_block, moved_mob, valid_cells)
    drive = 0.25 * dos[:, None, None]
    out_even = mixed[0] + 0.08 * lap[0] + drive * mixed[1]
    out_odd = mixed[1] + 0.08 * lap[1] - drive * mixed[0]
    return jnp.stack([out_even, out_odd])


def solution(mesh):
    in_specs = (
        P(None, "egrp", "space", None),
        P(None, None, "egrp", "space", None),
        P(None, None, "egrp", "space", None),
        P("space", None),
        P("space", None),
        P(),
        P(),
        P(),
    )
    out_specs = P(None, "egrp", "space", None)
    return jax.shard_map(local, mesh=mesh, in_specs=in_specs, out_specs=out_specs, check_vma=False)
```

profile of v0, /device:TPU:11, one launch (start us, length us, event | category | flops | bytes accessed | tf_op | source)
XLA Modules:
  0.0 195.8 jit_solution(16239742261708099260)
XLA Ops:
  0.0 1.7 fusion.84
  1.7 1.4 copy.175
  3.1 3.8 %all-to-all-start = ((f32[512,2,256]{0,2,1:T(8,128)}), f32[512,2,256]{0,2,1:T(8,128)S(1)}, u32[]{:S(2)}, u32[]{:S(2)}) async-start(f32[512,2,256]{0,2,1:T(8,128)} %bitcast.6), calls=%async_computation | async-start | bytes 2097152 | tf_op jit(solution)/shard_map/all_to_all | solution.py:52
  6.9 4.0 %collective-permute-start = (f32[1,1,1,128]{3,2,1,0:T(1,128)S(1)}, f32[1,1,1,128]{3,2,1,0:T(1,128)S(1)}, u32[]{:S(2)}, u32[]{:S(2)}) collective-permute-start(f32[1,1,1,128]{3,2,1,0:T(1,128)S(1)} %get-tuple-element.53), channel_id=1, source_target_pairs={{0,1},{1,2},{2,3},{3,4},{4,5},{5,6},{6,7},{7,8},{8,9},{9,10},{10,1... | collective-permute-start | bytes 1544 | tf_op jit(solution)/shard_map/ppermute | solution.py:18
  10.9 1.9 collective-permute-start.2
  12.9 0.7 fusion.90
  23.6 5.1 %reshape.555 = bf16[4,2,262144]{2,1,0:T(2,128)(2,1)} reshape(bf16[4,2,512,4,128]{4,3,2,1,0:T(4,128)(2,1)} %param.13) | data formatting | bytes 8388608 | tf_op jit(solution)/shard_map/reshape | solution.py:34
  28.7 4.1 %fusion.83 = (bf16[1,1,512,4,128]{4,3,2,1,0:T(4,128)(2,1)}, bf16[1,1,512,4,128]{4,3,2,1,0:T(4,128)(2,1)}, bf16[1,1,512,4,128]{4,3,2,1,0:T(4,128)(2,1)}, bf16[1,1...) fusion(bf16[4,2,512,4,128]{4,3,2,1,0:T(4,128)(2,1)} %param.13), kind=kLoop, calls=%fused_computation.196 | loop fusion | bytes 8388608 | tf_op jit(solution)/shard_map/slice | solution.py:97
  33.1 0.7 fusion.89
  33.7 2.5 %add_multiply_fusion.2 = (f32[512]{0:T(512)S(1)}, f32[512]{0:T(512)S(1)}) fusion(s32[]{:T(128)} %bitcast.10, f32[]{:T(128)} %bitcast.2, s32[]{:T(128)S(6)} %mul.605, s32[]{:T(128)} %bitcast.9, f32[]{:T(128)} %bitcast.1), kind=kLoop, calls=%fused_computation.143 | loop fusion | flops 17920 | bytes 4116 | tf_op jit(solution)/shard_map/mul | solution.py:49
  36.2 2.5 %add_multiply_fusion = (f32[512]{0:T(512)S(1)}, f32[512]{0:T(512)S(1)}) fusion(s32[]{:T(128)} %bitcast.12, f32[]{:T(128)} %bitcast.4, s32[]{:T(128)S(6)} %mul.605, s32[]{:T(128)} %bitcast.11, f32[]{:T(128)} %bitcast.3), kind=kLoop, calls=%fused_computation.141 | loop fusion | flops 17920 | bytes 4116 | tf_op jit(solution)/shard_map/mul | solution.py:49
  38.7 2.4 %select_select_fusion.2 = (f32[4,128]{1,0:T(4,128)S(1)}, pred[4,128]{1,0:T(4,128)(4,1)S(1)}, pred[4,128]{1,0:T(4,128)(4,1)S(1)}, pred[4,128]{1,0:T(4,128)(4,1)S(1)}, pred[4,128]{1,0:T(4,128)(4,1)S(1)}) fusion(f32[]{:T(128)} %bitcast.4, f32[]{:T(128)} %bitcast.3, f32[]{:T(128)} %bitcast.2, f32[]{:T(128)} %bitcast.1, s32[4,128]{1,0:T(4,128)S(1)} %copy-done.22), kind=kLoop, calls=%fused_computation.163 | loop fusion | flops 4096 | bytes 6160 | tf_op jit(solution)/shard_map/jit(_where)/select_n | solution.py:51
  41.5 4.1 %fusion.82 = (bf16[1,1,512,4,128]{4,3,2,1,0:T(4,128)(2,1)}, bf16[1,1,512,4,128]{4,3,2,1,0:T(4,128)(2,1)}, bf16[1,1,512,4,128]{4,3,2,1,0:T(4,128)(2,1)}, bf16[1,1...) fusion(bf16[4,2,512,4,128]{4,3,2,1,0:T(4,128)(2,1)} %param.12), kind=kLoop, calls=%fused_computation.195 | loop fusion | bytes 8388608 | tf_op jit(solution)/shard_map/slice | solution.py:96
  45.7 2.2 %copy.185 = bf16[1,1,512,4,128]{2,4,3,1,0:T(8,128)(2,1)} copy(bf16[1,1,512,4,128]{4,3,2,1,0:T(4,128)(2,1)} %get-tuple-element.22) | data formatting | bytes 1048576
  47.9 1.1 copy.186
  49.0 2.1 %copy.187 = bf16[1,1,512,4,128]{2,4,3,1,0:T(8,128)(2,1)} copy(bf16[1,1,512,4,128]{4,3,2,1,0:T(4,128)(2,1)} %get-tuple-element.21) | data formatting | bytes 1048576
  51.1 1.1 copy.188
  52.2 2.2 %copy.189 = bf16[1,1,512,4,128]{2,4,3,1,0:T(8,128)(2,1)} copy(bf16[1,1,512,4,128]{4,3,2,1,0:T(4,128)(2,1)} %get-tuple-element.20) | data formatting | bytes 1048576
  54.4 2.2 %copy.190 = bf16[1,1,512,4,128]{2,4,3,1,0:T(8,128)(2,1)} copy(bf16[1,1,512,4,128]{4,3,2,1,0:T(4,128)(2,1)} %get-tuple-element.28) | data formatting | bytes 1048576
  56.6 2.1 %copy.191 = bf16[1,1,512,4,128]{2,4,3,1,0:T(8,128)(2,1)} copy(bf16[1,1,512,4,128]{4,3,2,1,0:T(4,128)(2,1)} %get-tuple-element.26) | data formatting | bytes 1048576
  58.7 1.2 copy.192
  59.8 2.2 %copy.177 = bf16[1,1,512,4,128]{2,4,3,1,0:T(8,128)(2,1)} copy(bf16[1,1,512,4,128]{4,3,2,1,0:T(4,128)(2,1)} %get-tuple-element.19) | data formatting | bytes 1048576
  62.0 1.2 copy.178
  63.2 1.1 copy.179
  65.0 2.3 %fusion.25 = f32[1024,256]{1,0:T(8,128)} fusion(s32[]{:T(128)S(6)} %select_n.228, f32[1024,256]{1,0:T(8,128)S(1)} %bitcast.141, s32[]{:T(128)S(6)} %select_n.229, s32[]{:T(128)S(6)} %select_n.230, s32[]{:T(128)S(6)} %select_n.231, s32[]{:T(128)S(6)} %select_n.232, s32[]{:T(128)S(6)} %select_n.233, s32[]{:T(128)S(6)} %select_n.234, s32[]{:T(128)S(6)} %select_n.235, ...), kind=kLoop, calls=%fused_computation.64 | loop fusion | flops 4194304 | bytes 2098208 | tf_op jit(solution)/shard_map/jit(_where)/select_n | solution.py:66
  67.3 3.8 %all-to-all-start.1 = ((f32[2,512,256]{2,1,0:T(8,128)}), f32[2,512,256]{2,1,0:T(8,128)S(1)}, u32[]{:S(2)}, u32[]{:S(2)}) async-start(f32[2,512,256]{2,1,0:T(8,128)} %bitcast.13), calls=%async_computation.1 | async-start | bytes 2097152 | tf_op jit(solution)/shard_map/all_to_all | solution.py:69
  71.1 9.5 %fusion = f32[2,4,4]{2,1,0:T(4,128)S(1)} fusion(bf16[4,2,262144]{2,1,0:T(2,128)(2,1)} %reshape.555), kind=kOutput, calls=%fused_computation.18 | convolution fusion | flops 16777216 | bytes 4194432 | tf_op jit(solution)/shard_map/dot_general | solution.py:79
  80.6 2.2 %copy.180 = bf16[1,1,512,4,128]{2,4,3,1,0:T(8,128)(2,1)} copy(bf16[1,1,512,4,128]{4,3,2,1,0:T(4,128)(2,1)} %get-tuple-element.33) | data formatting | bytes 1048576
  82.8 2.1 %copy.181 = bf16[1,1,512,4,128]{2,4,3,1,0:T(8,128)(2,1)} copy(bf16[1,1,512,4,128]{4,3,2,1,0:T(4,128)(2,1)} %get-tuple-element.24) | data formatting | bytes 1048576
  84.9 1.1 copy.182
  86.0 2.1 %copy.183 = bf16[1,1,512,4,128]{2,4,3,1,0:T(8,128)(2,1)} copy(bf16[1,1,512,4,128]{4,3,2,1,0:T(4,128)(2,1)} %get-tuple-element.23) | data formatting | bytes 1048576
  88.1 1.1 copy.184
  89.3 1.3 copy.141
  90.6 2.3 %divide_subtract_fusion.1 = (f32[1,512,4,128]{1,3,2,0:T(8,128)S(1)}, f32[1,512,4,128]{1,3,2,0:T(8,128)S(1)}) fusion(f32[1,512,4,128]{1,3,2,0:T(8,128)} %copy.175, f32[1,512,4,128]{1,3,2,0:T(8,128)} %bitcast.146, f32[512]{0:T(512)S(1)} %get-tuple-element.98, f32[512]{0:T(512)S(1)} %get-tuple-element.99, f32[512]{0:T(512)S(1)} %get-tuple-element.100, ...), kind=kLoop, calls=%fused_computation.94 | loop fusion | flops 3407872 | bytes 5257216 | tf_op jit(solution)/shard_map/sub | solution.py:75
  92.9 1.3 copy.142
  94.2 1.3 copy.144
  95.6 1.6 pad_maximum_fusion.5
  97.2 2.9 %copy.145 = f32[2,512,4,128]{3,2,1,0:T(4,128)} copy(f32[2,512,4,128]{1,3,2,0:T(8,128)} %pad_maximum_fusion.5) | data formatting | bytes 4194304 | tf_op jit(solution)/shard_map/stack | solution.py:75
  100.1 5.3 %multiply_reduce_fusion = f32[4,2]{1,0:T(4,128)S(1)} fusion(bf16[4,2,512,4,128]{4,3,2,1,0:T(4,128)(2,1)} %param.13, f32[2,512,4,128]{3,2,1,0:T(4,128)} %copy.145), kind=kLoop, calls=%fused_computation | loop fusion | flops 6291448 | bytes 6291488 | tf_op jit(solution)/shard_map/reduce_sum | solution.py:77
  105.4 2.3 %fusion.15 = f32[2]{0:T(128)S(1)} fusion(f32[1,262144]{1,0:T(1,128)S(1)} %bitcast.143, f32[1,262144]{1,0:T(1,128)S(1)} %bitcast.142), kind=kLoop, calls=%fused_computation.38 | loop fusion | flops 1572862 | bytes 2097160 | tf_op jit(solution)/shard_map/reduce_sum | solution.py:78
  107.7 40.7 %all-reduce.1 = (f32[2,4,4]{2,1,0:T(4,128)S(1)}, f32[2,4]{0,1:T(4,128)S(1)}, f32[2]{0:T(128)S(1)}) all-reduce(f32[2,4,4]{2,1,0:T(4,128)S(1)} %fusion, f32[2,4]{0,1:T(4,128)S(1)} %bitcast.152, f32[2]{0:T(128)S(1)} %fusion.15), channel_id=1, replica_groups=mesh['egrp'=2,'space'=16] {'egrp','space'}, use_global_device_ids=true, to_apply=%region_4.5 | all-reduce | flops 42 | bytes 336 | tf_op jit(solution)/shard_map/psum | solution.py:82
  148.5 0.6 fusion.87
  149.3 0.7 maximum_bitcast_fusion.1
  150.9 0.7 compare_reduce_fusion
  151.6 0.6 fusion.50
  152.8 0.8 fusion.92
  153.6 0.6 broadcast_divide_fusion
  154.2 0.6 fusion.88
  154.9 0.7 maximum_bitcast_fusion
  156.6 0.6 compare_reduce_fusion.1
  157.2 0.6 fusion.49
  158.5 0.8 fusion.91
  159.2 0.6 broadcast_divide_fusion.1
  159.9 0.7 fusion.86
  160.6 6.4 %bitcast_add_fusion = f32[1,512,4,128]{1,3,2,0:T(8,128)S(1)} fusion(bf16[1,1,512,4,128]{2,4,3,1,0:T(8,128)(2,1)} %copy.192, bf16[1,1,512,4,128]{2,4,3,1,0:T(8,128)(2,1)} %copy.191, bf16[1,1,512,4,128]{2,4,3,1,0:T(8,128)(2,1)} %copy.190, bf16[1,1,512,4,128]{2,4,3,1,0:T(8,128)(2,1)} %copy.189, bf16[1,1,512,4,128]{2,4,3,1,0:T(8,128)(2,1)} %copy.188, ...), kind=kLoop, calls=%fused_computation.86 | loop fusion | flops 9175040 | bytes 6303764 | tf_op jit(solution)/shard_map/add | solution.py:95
  167.1 5.4 %bitcast_add_fusion.4 = f32[1,512,4,128]{1,3,2,0:T(8,128)S(1)} fusion(bf16[1,1,512,4,128]{2,4,3,1,0:T(8,128)(2,1)S(1)} %copy-done.18, bf16[1,1,512,4,128]{2,4,3,1,0:T(8,128)(2,1)S(1)} %copy-done.17, bf16[1,1,512,4,128]{2,4,3,1,0:T(8,128)(2,1)S(1)} %copy-done.16, bf16[1,1,512,4,128]{2,4,3,1,0:T(8,128)(2,1)S(1)} %copy-done.15, ...), kind=kLoop, calls=%fused_computation.90 | loop fusion | flops 7077888 | bytes 7340052 | tf_op jit(solution)/shard_map/add | solution.py:95
  172.5 4.5 %collective-permute-start.1 = (f32[2,512,1,128]{1,3,2,0:T(8,128)S(1)}, f32[2,512,1,128]{1,3,2,0:T(8,128)S(1)}, u32[]{:S(2)}, u32[]{:S(2)}) collective-permute-start(f32[2,512,1,128]{1,3,2,0:T(8,128)S(1)} %get-tuple-element.41), channel_id=1, source_target_pairs={{0,1},{1,2},{2,3},{3,4},{4,5},{5,6},{6,7},{7,8},{8,9},{9,10},{10,1... | collective-permute-start | bytes 1572872 | tf_op jit(solution)/shard_map/ppermute | solution.py:18
  177.0 1.9 collective-permute-start.3
  179.2 0.5 fusion.3
  179.7 9.0 %collective-permute-done.1 = f32[2,512,1,128]{1,3,2,0:T(8,128)S(1)} collective-permute-done((f32[2,512,1,128]{1,3,2,0:T(8,128)S(1)}, f32[2,512,1,128]{1,3,2,0:T(8,128)S(1)}, u32[]{:S(2)}, u32[]{:S(2)}) %collective-permute-start.1) | collective-permute-done | bytes 524320 | tf_op jit(solution)/shard_map/ppermute | solution.py:18
  188.7 1.6 collective-permute-done.3
  190.3 2.9 %fusion.11 = f32[2,512,4,128]{1,3,2,0:T(8,128)S(1)} fusion(f32[2,512,1,128]{1,3,2,0:T(8,128)S(1)} %collective-permute-done.3, f32[1,512,4,128]{1,3,2,0:T(8,128)S(1)} %bitcast_add_fusion, f32[1,512,4,128]{1,3,2,0:T(8,128)S(1)} %bitcast_add_fusion.4, f32[2,512,1,128]{1,3,2,0:T(8,128)S(1)} %collective-permute-done.1, ...), kind=kLoop, calls=%fused_computation.30 | loop fusion | flops 15204352 | bytes 11545096 | tf_op jit(solution)/shard_map/add | solution.py:27
  193.2 0.5 fusion.44
  194.0 1.8 copy.174
  (93 shorter events, 5.2 us)
Async XLA Ops:
  1.7 5.3 %copy-start.19 = (f32[4,128]{1,0:T(4,128)S(1)}, f32[4,128]{1,0:T(4,128)}, u32[]{:S(2)}) copy-start(f32[4,128]{1,0:T(4,128)} %param.14) | copy-start | bytes 6148
  1.7 11.2 %copy-start.20 = (s32[4]{0:T(128)S(1)}, s32[4]{0:T(128)}, u32[]{:S(2)}) copy-start(s32[4]{0:T(128)} %param.16) | copy-start | bytes 52
  3.1 61.6 %all-to-all-start = ((f32[512,2,256]{0,2,1:T(8,128)}), f32[512,2,256]{0,2,1:T(8,128)S(1)}, u32[]{:S(2)}, u32[]{:S(2)}) async-start(f32[512,2,256]{0,2,1:T(8,128)} %bitcast.6), calls=%async_computation | async-start | bytes 2097152 | tf_op jit(solution)/shard_map/all_to_all | solution.py:52
  6.9 82.3 %collective-permute-start = (f32[1,1,1,128]{3,2,1,0:T(1,128)S(1)}, f32[1,1,1,128]{3,2,1,0:T(1,128)S(1)}, u32[]{:S(2)}, u32[]{:S(2)}) collective-permute-start(f32[1,1,1,128]{3,2,1,0:T(1,128)S(1)} %get-tuple-element.53), channel_id=1, source_target_pairs={{0,1},{1,2},{2,3},{3,4},{4,5},{5,6},{6,7},{7,8},{8,9},{9,10},{10,1... | collective-permute-start | bytes 1544 | tf_op jit(solution)/shard_map/ppermute | solution.py:18
  10.9 78.3 %collective-permute-start.2 = (f32[1,1,1,128]{3,2,1,0:T(1,128)S(1)}, f32[1,1,1,128]{3,2,1,0:T(1,128)S(1)}, u32[]{:S(2)}, u32[]{:S(2)}) collective-permute-start(f32[1,1,1,128]{3,2,1,0:T(1,128)S(1)} %get-tuple-element.54), channel_id=1, source_target_pairs={{1,0},{2,1},{3,2},{4,3},{5,4},{6,5},{7,6},{8,7},{9,8},{10,9},{11,1... | collective-permute-start | bytes 1544 | tf_op jit(solution)/shard_map/ppermute | solution.py:21
  28.7 4.3 %copy-start.21 = (f32[4]{0:T(128)S(1)}, f32[4]{0:T(128)}, u32[]{:S(2)}) copy-start(f32[4]{0:T(128)} %param.17) | copy-start | bytes 52
  28.7 10.0 %copy-start.22 = (s32[4,128]{1,0:T(4,128)S(1)}, s32[4,128]{1,0:T(4,128)}, u32[]{:S(2)}) copy-start(s32[4,128]{1,0:T(4,128)} %param.15) | copy-start | bytes 6148
  32.8 8.7 %copy-start.23 = (s32[2,4]{1,0:T(2,128)S(1)}, s32[2,4]{1,0:T(2,128)}, u32[]{:S(2)}) copy-start(s32[2,4]{1,0:T(2,128)} %param.18) | copy-start | bytes 100
  41.5 6.3 %copy-start.7 = (bf16[1,1,512,4,128]{4,3,2,1,0:T(4,128)(2,1)S(1)}, bf16[1,1,512,4,128]{4,3,2,1,0:T(4,128)(2,1)}, u32[]{:S(2)}) copy-start(bf16[1,1,512,4,128]{4,3,2,1,0:T(4,128)(2,1)} %get-tuple-element.30) | copy-start | bytes 1572868
  45.7 5.4 %copy-start.6 = (bf16[1,1,512,4,128]{4,3,2,1,0:T(4,128)(2,1)S(1)}, bf16[1,1,512,4,128]{4,3,2,1,0:T(4,128)(2,1)}, u32[]{:S(2)}) copy-start(bf16[1,1,512,4,128]{4,3,2,1,0:T(4,128)(2,1)} %get-tuple-element.29) | copy-start | bytes 1572868
  51.1 7.6 %copy-start.5 = (bf16[1,1,512,4,128]{4,3,2,1,0:T(4,128)(2,1)S(1)}, bf16[1,1,512,4,128]{4,3,2,1,0:T(4,128)(2,1)}, u32[]{:S(2)}) copy-start(bf16[1,1,512,4,128]{4,3,2,1,0:T(4,128)(2,1)} %get-tuple-element.34) | copy-start | bytes 1572868
  54.4 7.7 %copy-start.4 = (bf16[1,1,512,4,128]{4,3,2,1,0:T(4,128)(2,1)S(1)}, bf16[1,1,512,4,128]{4,3,2,1,0:T(4,128)(2,1)}, u32[]{:S(2)}) copy-start(bf16[1,1,512,4,128]{4,3,2,1,0:T(4,128)(2,1)} %get-tuple-element.27) | copy-start | bytes 1572868
  59.8 3.4 %copy-start.8 = (bf16[1,1,512,4,128]{4,3,2,1,0:T(4,128)(2,1)S(1)}, bf16[1,1,512,4,128]{4,3,2,1,0:T(4,128)(2,1)}, u32[]{:S(2)}) copy-start(bf16[1,1,512,4,128]{4,3,2,1,0:T(4,128)(2,1)} %get-tuple-element.25) | copy-start | bytes 1572868
  67.3 22.0 %all-to-all-start.1 = ((f32[2,512,256]{2,1,0:T(8,128)}), f32[2,512,256]{2,1,0:T(8,128)S(1)}, u32[]{:S(2)}, u32[]{:S(2)}) async-start(f32[2,512,256]{2,1,0:T(8,128)} %bitcast.13), calls=%async_computation.1 | async-start | bytes 2097152 | tf_op jit(solution)/shard_map/all_to_all | solution.py:69
  80.6 4.3 %copy-start.3 = (bf16[1,1,512,4,128]{4,3,2,1,0:T(4,128)(2,1)S(1)}, bf16[1,1,512,4,128]{4,3,2,1,0:T(4,128)(2,1)}, u32[]{:S(2)}) copy-start(bf16[1,1,512,4,128]{4,3,2,1,0:T(4,128)(2,1)} %get-tuple-element.32) | copy-start | bytes 1572868
  80.6 7.5 %copy-start.2 = (bf16[1,1,512,4,128]{4,3,2,1,0:T(4,128)(2,1)S(1)}, bf16[1,1,512,4,128]{4,3,2,1,0:T(4,128)(2,1)}, u32[]{:S(2)}) copy-start(bf16[1,1,512,4,128]{4,3,2,1,0:T(4,128)(2,1)} %get-tuple-element.31) | copy-start | bytes 1572868
  100.1 5.3 %copy-start = (f32[1,512,4,128]{3,2,1,0:T(4,128)S(1)}, f32[1,512,4,128]{3,2,1,0:T(4,128)}, u32[]{:S(2)}) copy-start(f32[1,512,4,128]{3,2,1,0:T(4,128)} %copy.142) | copy-start | bytes 3145732
  100.1 5.3 %copy-start.1 = (f32[1,512,4,128]{3,2,1,0:T(4,128)S(1)}, f32[1,512,4,128]{3,2,1,0:T(4,128)}, u32[]{:S(2)}) copy-start(f32[1,512,4,128]{3,2,1,0:T(4,128)} %copy.144) | copy-start | bytes 3145732
  105.4 55.1 %copy-start.9 = (bf16[1,1,512,4,128]{2,4,3,1,0:T(8,128)(2,1)S(1)}, bf16[1,1,512,4,128]{2,4,3,1,0:T(8,128)(2,1)}, u32[]{:S(2)}) copy-start(bf16[1,1,512,4,128]{2,4,3,1,0:T(8,128)(2,1)} %copy.185) | copy-start | bytes 1572868
  105.4 55.1 %copy-start.11 = (bf16[1,1,512,4,128]{2,4,3,1,0:T(8,128)(2,1)S(1)}, bf16[1,1,512,4,128]{2,4,3,1,0:T(8,128)(2,1)}, u32[]{:S(2)}) copy-start(bf16[1,1,512,4,128]{2,4,3,1,0:T(8,128)(2,1)} %copy.186) | copy-start | bytes 1572868
  160.6 6.4 %copy-start.10 = (bf16[1,1,512,4,128]{2,4,3,1,0:T(8,128)(2,1)S(1)}, bf16[1,1,512,4,128]{2,4,3,1,0:T(8,128)(2,1)}, u32[]{:S(2)}) copy-start(bf16[1,1,512,4,128]{2,4,3,1,0:T(8,128)(2,1)} %copy.177) | copy-start | bytes 1572868
  160.6 6.4 %copy-start.12 = (bf16[1,1,512,4,128]{2,4,3,1,0:T(8,128)(2,1)S(1)}, bf16[1,1,512,4,128]{2,4,3,1,0:T(8,128)(2,1)}, u32[]{:S(2)}) copy-start(bf16[1,1,512,4,128]{2,4,3,1,0:T(8,128)(2,1)} %copy.178) | copy-start | bytes 1572868
  160.6 6.4 %copy-start.13 = (bf16[1,1,512,4,128]{2,4,3,1,0:T(8,128)(2,1)S(1)}, bf16[1,1,512,4,128]{2,4,3,1,0:T(8,128)(2,1)}, u32[]{:S(2)}) copy-start(bf16[1,1,512,4,128]{2,4,3,1,0:T(8,128)(2,1)} %copy.179) | copy-start | bytes 1572868
  160.6 6.4 %copy-start.14 = (bf16[1,1,512,4,128]{2,4,3,1,0:T(8,128)(2,1)S(1)}, bf16[1,1,512,4,128]{2,4,3,1,0:T(8,128)(2,1)}, u32[]{:S(2)}) copy-start(bf16[1,1,512,4,128]{2,4,3,1,0:T(8,128)(2,1)} %copy.180) | copy-start | bytes 1572868
  160.6 6.4 %copy-start.15 = (bf16[1,1,512,4,128]{2,4,3,1,0:T(8,128)(2,1)S(1)}, bf16[1,1,512,4,128]{2,4,3,1,0:T(8,128)(2,1)}, u32[]{:S(2)}) copy-start(bf16[1,1,512,4,128]{2,4,3,1,0:T(8,128)(2,1)} %copy.181) | copy-start | bytes 1572868
  160.6 6.4 %copy-start.16 = (bf16[1,1,512,4,128]{2,4,3,1,0:T(8,128)(2,1)S(1)}, bf16[1,1,512,4,128]{2,4,3,1,0:T(8,128)(2,1)}, u32[]{:S(2)}) copy-start(bf16[1,1,512,4,128]{2,4,3,1,0:T(8,128)(2,1)} %copy.182) | copy-start | bytes 1572868
  160.6 6.4 %copy-start.17 = (bf16[1,1,512,4,128]{2,4,3,1,0:T(8,128)(2,1)S(1)}, bf16[1,1,512,4,128]{2,4,3,1,0:T(8,128)(2,1)}, u32[]{:S(2)}) copy-start(bf16[1,1,512,4,128]{2,4,3,1,0:T(8,128)(2,1)} %copy.183) | copy-start | bytes 1572868
  160.6 6.4 %copy-start.18 = (bf16[1,1,512,4,128]{2,4,3,1,0:T(8,128)(2,1)S(1)}, bf16[1,1,512,4,128]{2,4,3,1,0:T(8,128)(2,1)}, u32[]{:S(2)}) copy-start(bf16[1,1,512,4,128]{2,4,3,1,0:T(8,128)(2,1)} %copy.184) | copy-start | bytes 1572868
  172.5 16.2 %collective-permute-start.1 = (f32[2,512,1,128]{1,3,2,0:T(8,128)S(1)}, f32[2,512,1,128]{1,3,2,0:T(8,128)S(1)}, u32[]{:S(2)}, u32[]{:S(2)}) collective-permute-start(f32[2,512,1,128]{1,3,2,0:T(8,128)S(1)} %get-tuple-element.41), channel_id=1, source_target_pairs={{0,1},{1,2},{2,3},{3,4},{4,5},{5,6},{6,7},{7,8},{8,9},{9,10},{10,1... | collective-permute-start | bytes 1572872 | tf_op jit(solution)/shard_map/ppermute | solution.py:18
  177.0 13.3 %collective-permute-start.3 = (f32[2,512,1,128]{1,3,2,0:T(8,128)S(1)}, f32[2,512,1,128]{1,3,2,0:T(8,128)S(1)}, u32[]{:S(2)}, u32[]{:S(2)}) collective-permute-start(f32[2,512,1,128]{1,3,2,0:T(8,128)S(1)} %get-tuple-element.42), channel_id=1, source_target_pairs={{1,0},{2,1},{3,2},{4,3},{5,4},{6,5},{7,6},{8,7},{9,8},{10,9},{11,1... | collective-permute-start | bytes 1572872 | tf_op jit(solution)/shard_map/ppermute | solution.py:21
where the time goes:
time: 197 us; the launch traced here: 196 us
  local copies, waits for them, and re-layouts  57.4 us (29%)
  other arithmetic  45.2 us (23%)
  blocking collectives  40.7 us (21%)
  starting transfers between devices  19.9 us (10%)
  matrix products  11.5 us (6%)
  waiting for transfers between devices  10.6 us (5%)
  between operations  10.6 us (5%)
    psum x1, blocking collectives, local(): lax.psum((among, cross, self_term), ('egrp', 'space'))  40.7 us
    unnamed x66, local copies, waits for them, and re-layouts  29.2 us
    add x2, other arithmetic, local(): part_mix + coeffs[index + 1] * (hist_x[index, field].astype(jnp.float32)...  11.7 us
    dot_general x1, matrix products, local(): lax.dot_general(flat_g, flat_g, (((2,), (2,)), ((1,), (1,))), preferred_e...  9.54 us
    ppermute x2, waiting for transfers between devices, extended(): lax.ppermute(lax.slice_in_dim(block, block.shape[dim] - width, None, axis...  9 us
    ppermute x2, starting transfers between devices, extended(): lax.ppermute(lax.slice_in_dim(block, block.shape[dim] - width, None, axis...  8.46 us
    reduce_sum x1, other arithmetic, local(): jnp.sum(flat_g.astype(jnp.float32) * res_flat[None], axis=2)  5.32 us
    reshape x1, local copies, waits for them, and re-layouts, local(): flat_g = hist_g.reshape(HISTORY, 2, -1)  5.11 us
  transfers between devices with their start and end apart: 6, of which 2 were waited for; matrix products, arithmetic and copies ran while one was open for 32% of the time, Pallas kernels for 0%

commit v1 on v0

--- a/solution.py
+++ b/solution.py
@@ -8,6 +8,14 @@
 NREGION = 4
 KMAX = 64
 COLS = 64
+
+
+def run_flows(work_x, axis_id):
+    block_out = jnp.split(work_x, lax.axis_size(axis_id), axis=1)
+    raw_out = jnp.stack(block_out)
+    heard = lax.all_to_all(raw_out, split_axis=0, axis_name=axis_id, concat_axis=0)
+    earlier = jnp.concatenate(heard, axis=0)
+    return earlier
 
 
 def extended(block, sides, width):
@@ -49,9 +57,7 @@
         rate = coupling[index] * (1.5 * dos_low + 0.5 * dos_high)
         outrate = jnp.where((region == index)[None], rate[:, None, None], outrate)
         lam = jnp.where(region == index, coupling[index], lam)
-    column = lax.all_to_all(
-        even.reshape(width, rows * cells), "egrp", split_axis=1, concat_axis=0, tiled=True
-    )
+    column = run_flows(even.reshape(width, rows * cells), "egrp")
     span = column.shape[1]
     column_region = lax.dynamic_slice_in_dim(
         region.reshape(-1), lax.axis_index("egrp") * span, span

time: 197 us -> 209 us (1.061)
  local copies, waits for them, and re-layouts: 57.4 us -> 66.7 us
    unnamed x66 -> x50, local copies, waits for them, and re-layouts: 29.2 us -> 36.2 us
  transfers between devices with their start and end apart: 6 -> 6, of which waited for: 2 -> 2; matrix products, arithmetic and copies ran while one was open for 32% -> 34% of each run, Pallas kernels for 0% -> 0%
where the time goes in v1:
time: 209 us; the launch traced here: 207 us
  local copies, waits for them, and re-layouts  66.7 us (32%)
  other arithmetic  47.1 us (23%)
  blocking collectives  40.7 us (19%)
  starting transfers between devices  19.9 us (10%)
  matrix products  11.5 us (6%)
  between operations  11 us (5%)
  waiting for transfers between devices  10.6 us (5%)
    psum x1, blocking collectives, local(): lax.psum((among, cross, self_term), ('egrp', 'space'))  40.7 us
    unnamed x50, local copies, waits for them, and re-layouts  36.2 us
    add x2, other arithmetic, local(): part_mix + coeffs[index + 1] * (hist_x[index, field].astype(jnp.float32)...  10.6 us
    dot_general x1, matrix products, local(): lax.dot_general(flat_g, flat_g, (((2,), (2,)), ((1,), (1,))), preferred_e...  9.54 us
    ppermute x2, waiting for transfers between devices, extended(): lax.ppermute(lax.slice_in_dim(block, block.shape[dim] - width, None, axis...  9 us
    ppermute x2, starting transfers between devices, extended(): lax.ppermute(lax.slice_in_dim(block, block.shape[dim] - width, None, axis...  8.46 us
    reduce_sum x1, other arithmetic, local(): jnp.sum(flat_g.astype(jnp.float32) * res_flat[None], axis=2)  5.32 us
    reshape x1, local copies, waits for them, and re-layouts, local(): flat_g = hist_g.reshape(HISTORY, 2, -1)  5.17 us
  transfers between devices with their start and end apart: 6, of which 2 were waited for; matrix products, arithmetic and copies ran while one was open for 34% of the time, Pallas kernels for 0%

profile of v1, /device:TPU:11, one launch (start us, length us, event | category | flops | bytes accessed | tf_op | source)
XLA Modules:
  0.0 207.4 jit_solution(7190393212575416732)
XLA Ops:
  0.0 2.6 %fusion.84 = (f32[1,512,4,128]{3,2,1,0:T(4,128)S(1)}, f32[1,512,4,128]{3,2,1,0:T(4,128)}) fusion(f32[2,512,4,128]{3,2,1,0:T(4,128)} %param.11), kind=kLoop, calls=%fused_computation.198 | loop fusion | bytes 4194304 | tf_op jit(solution)/shard_map/slice | solution.py:45
  3.5 1.0 pad_maximum_fusion.7
  4.6 3.8 %all-to-all-start = ((f32[2,512,256]{2,1,0:T(8,128)}), f32[2,512,256]{2,1,0:T(8,128)S(1)}, u32[]{:S(2)}, u32[]{:S(2)}) async-start(f32[2,512,256]{2,1,0:T(8,128)} %pad_maximum_fusion.7), calls=%async_computation | async-start | bytes 2097152 | tf_op jit(solution)/shard_map/all_to_all | solution.py:16
  8.4 4.0 %collective-permute-start = (f32[1,1,1,128]{3,2,1,0:T(1,128)S(1)}, f32[1,1,1,128]{3,2,1,0:T(1,128)S(1)}, u32[]{:S(2)}, u32[]{:S(2)}) collective-permute-start(f32[1,1,1,128]{3,2,1,0:T(1,128)S(1)} %get-tuple-element.55), channel_id=1, source_target_pairs={{0,1},{1,2},{2,3},{3,4},{4,5},{5,6},{6,7},{7,8},{8,9},{9,10},{10,1... | collective-permute-start | bytes 1544 | tf_op jit(solution)/shard_map/ppermute | solution.py:26
  12.4 1.9 collective-permute-start.2
  14.3 0.7 fusion.91
  25.5 5.2 %reshape.555 = bf16[4,2,262144]{2,1,0:T(2,128)(2,1)} reshape(bf16[4,2,512,4,128]{4,3,2,1,0:T(4,128)(2,1)} %param.13) | data formatting | bytes 8388608 | tf_op jit(solution)/shard_map/reshape | solution.py:42
  30.6 4.2 %fusion.83 = (bf16[1,1,512,4,128]{4,3,2,1,0:T(4,128)(2,1)}, bf16[1,1,512,4,128]{4,3,2,1,0:T(4,128)(2,1)}, bf16[1,1,512,4,128]{4,3,2,1,0:T(4,128)(2,1)}, bf16[1,1...) fusion(bf16[4,2,512,4,128]{4,3,2,1,0:T(4,128)(2,1)} %param.13), kind=kLoop, calls=%fused_computation.197 | loop fusion | bytes 8388608 | tf_op jit(solution)/shard_map/slice | solution.py:103
  35.1 0.7 fusion.90
  35.7 2.6 %add_multiply_fusion = (f32[512]{0:T(512)S(1)}, f32[512]{0:T(512)S(1)}) fusion(s32[]{:T(128)} %bitcast.13, f32[]{:T(128)} %bitcast.4, s32[]{:T(128)S(6)} %mul.605, s32[]{:T(128)} %bitcast.12, f32[]{:T(128)} %bitcast.3), kind=kLoop, calls=%fused_computation.142 | loop fusion | flops 17920 | bytes 4116 | tf_op jit(solution)/shard_map/mul | solution.py:57
  38.4 2.5 %add_multiply_fusion.2 = (f32[512]{0:T(512)S(1)}, f32[512]{0:T(512)S(1)}) fusion(s32[]{:T(128)} %bitcast.11, f32[]{:T(128)} %bitcast.2, s32[]{:T(128)S(6)} %mul.605, s32[]{:T(128)} %bitcast.10, f32[]{:T(128)} %bitcast.1), kind=kLoop, calls=%fused_computation.144 | loop fusion | flops 17920 | bytes 4116 | tf_op jit(solution)/shard_map/mul | solution.py:57
  40.9 2.5 %select_select_fusion.2 = (f32[4,128]{1,0:T(4,128)S(1)}, pred[4,128]{1,0:T(4,128)(4,1)S(1)}, pred[4,128]{1,0:T(4,128)(4,1)S(1)}, pred[4,128]{1,0:T(4,128)(4,1)S(1)}, pred[4,128]{1,0:T(4,128)(4,1)S(1)}) fusion(f32[]{:T(128)} %bitcast.4, f32[]{:T(128)} %bitcast.3, f32[]{:T(128)} %bitcast.2, f32[]{:T(128)} %bitcast.1, s32[4,128]{1,0:T(4,128)S(1)} %copy-done.13), kind=kLoop, calls=%fused_computation.164 | loop fusion | flops 4096 | bytes 6160 | tf_op jit(solution)/shard_map/jit(_where)/select_n | solution.py:59
  43.4 1.6 copy.182
  45.0 4.1 %fusion.82 = (bf16[1,1,512,4,128]{4,3,2,1,0:T(4,128)(2,1)}, bf16[1,1,512,4,128]{4,3,2,1,0:T(4,128)(2,1)}, bf16[1,1,512,4,128]{4,3,2,1,0:T(4,128)(2,1)}, bf16[1,1...) fusion(bf16[4,2,512,4,128]{4,3,2,1,0:T(4,128)(2,1)} %param.12), kind=kLoop, calls=%fused_computation.196 | loop fusion | bytes 8388608 | tf_op jit(solution)/shard_map/slice | solution.py:102
  49.0 2.1 %copy.191 = bf16[1,1,512,4,128]{2,4,3,1,0:T(8,128)(2,1)} copy(bf16[1,1,512,4,128]{4,3,2,1,0:T(4,128)(2,1)} %get-tuple-element.22) | data formatting | bytes 1048576
  51.1 2.1 %copy.192 = bf16[1,1,512,4,128]{2,4,3,1,0:T(8,128)(2,1)} copy(bf16[1,1,512,4,128]{4,3,2,1,0:T(4,128)(2,1)} %get-tuple-element.30) | data formatting | bytes 1048576
  53.2 2.1 %copy.193 = bf16[1,1,512,4,128]{2,4,3,1,0:T(8,128)(2,1)} copy(bf16[1,1,512,4,128]{4,3,2,1,0:T(4,128)(2,1)} %get-tuple-element.21) | data formatting | bytes 1048576
  55.4 2.1 %copy.194 = bf16[1,1,512,4,128]{2,4,3,1,0:T(8,128)(2,1)} copy(bf16[1,1,512,4,128]{4,3,2,1,0:T(4,128)(2,1)} %get-tuple-element.29) | data formatting | bytes 1048576
  57.5 2.1 %copy.195 = bf16[1,1,512,4,128]{2,4,3,1,0:T(8,128)(2,1)} copy(bf16[1,1,512,4,128]{4,3,2,1,0:T(4,128)(2,1)} %get-tuple-element.20) | data formatting | bytes 1048576
  59.6 2.1 %copy.196 = bf16[1,1,512,4,128]{2,4,3,1,0:T(8,128)(2,1)} copy(bf16[1,1,512,4,128]{4,3,2,1,0:T(4,128)(2,1)} %get-tuple-element.28) | data formatting | bytes 1048576
  61.7 2.1 %copy.197 = bf16[1,1,512,4,128]{2,4,3,1,0:T(8,128)(2,1)} copy(bf16[1,1,512,4,128]{4,3,2,1,0:T(4,128)(2,1)} %get-tuple-element.26) | data formatting | bytes 1048576
  63.8 2.1 %copy.198 = bf16[1,1,512,4,128]{2,4,3,1,0:T(8,128)(2,1)} copy(bf16[1,1,512,4,128]{4,3,2,1,0:T(4,128)(2,1)} %get-tuple-element.34) | data formatting | bytes 1048576
  65.9 2.1 %copy.183 = bf16[1,1,512,4,128]{2,4,3,1,0:T(8,128)(2,1)} copy(bf16[1,1,512,4,128]{4,3,2,1,0:T(4,128)(2,1)} %get-tuple-element.19) | data formatting | bytes 1048576
  68.0 2.1 %copy.184 = bf16[1,1,512,4,128]{2,4,3,1,0:T(8,128)(2,1)} copy(bf16[1,1,512,4,128]{4,3,2,1,0:T(4,128)(2,1)} %get-tuple-element.27) | data formatting | bytes 1048576
  70.2 2.1 %copy.185 = bf16[1,1,512,4,128]{2,4,3,1,0:T(8,128)(2,1)} copy(bf16[1,1,512,4,128]{4,3,2,1,0:T(4,128)(2,1)} %get-tuple-element.25) | data formatting | bytes 1048576
  72.6 2.3 %fusion.25 = f32[1024,256]{1,0:T(8,128)} fusion(s32[]{:T(128)S(6)} %select_n.228, f32[1024,256]{1,0:T(8,128)S(1)} %bitcast.143, s32[]{:T(128)S(6)} %select_n.229, s32[]{:T(128)S(6)} %select_n.230, s32[]{:T(128)S(6)} %select_n.231, s32[]{:T(128)S(6)} %select_n.232, s32[]{:T(128)S(6)} %select_n.233, s32[]{:T(128)S(6)} %select_n.234, s32[]{:T(128)S(6)} %select_n.235, ...), kind=kLoop, calls=%fused_computation.64 | loop fusion | flops 4194304 | bytes 2098208 | tf_op jit(solution)/shard_map/jit(_where)/select_n | solution.py:72
  74.8 3.8 %all-to-all-start.1 = ((f32[2,512,256]{2,1,0:T(8,128)}), f32[2,512,256]{2,1,0:T(8,128)S(1)}, u32[]{:S(2)}, u32[]{:S(2)}) async-start(f32[2,512,256]{2,1,0:T(8,128)} %bitcast.144), calls=%async_computation.1 | async-start | bytes 2097152 | tf_op jit(solution)/shard_map/all_to_all | solution.py:75
  78.6 9.5 %fusion = f32[2,4,4]{2,1,0:T(4,128)S(1)} fusion(bf16[4,2,262144]{2,1,0:T(2,128)(2,1)} %reshape.555), kind=kOutput, calls=%fused_computation.18 | convolution fusion | flops 16777216 | bytes 4194432 | tf_op jit(solution)/shard_map/dot_general | solution.py:85
  88.1 2.1 %copy.186 = bf16[1,1,512,4,128]{2,4,3,1,0:T(8,128)(2,1)} copy(bf16[1,1,512,4,128]{4,3,2,1,0:T(4,128)(2,1)} %get-tuple-element.33) | data formatting | bytes 1048576
  90.3 2.1 %copy.187 = bf16[1,1,512,4,128]{2,4,3,1,0:T(8,128)(2,1)} copy(bf16[1,1,512,4,128]{4,3,2,1,0:T(4,128)(2,1)} %get-tuple-element.24) | data formatting | bytes 1048576
  92.4 2.1 %copy.188 = bf16[1,1,512,4,128]{2,4,3,1,0:T(8,128)(2,1)} copy(bf16[1,1,512,4,128]{4,3,2,1,0:T(4,128)(2,1)} %get-tuple-element.32) | data formatting | bytes 1048576
  94.5 2.1 %copy.189 = bf16[1,1,512,4,128]{2,4,3,1,0:T(8,128)(2,1)} copy(bf16[1,1,512,4,128]{4,3,2,1,0:T(4,128)(2,1)} %get-tuple-element.23) | data formatting | bytes 1048576
  96.6 2.1 %copy.190 = bf16[1,1,512,4,128]{2,4,3,1,0:T(8,128)(2,1)} copy(bf16[1,1,512,4,128]{4,3,2,1,0:T(4,128)(2,1)} %get-tuple-element.31) | data formatting | bytes 1048576
  98.8 1.3 copy.145
  100.1 2.9 %divide_subtract_fusion.1 = (f32[1,512,4,128]{1,3,2,0:T(8,128)S(1)}, f32[1,512,4,128]{1,3,2,0:T(8,128)}) fusion(f32[1,512,4,128]{1,3,2,0:T(8,128)S(1)} %copy.179, f32[1,512,4,128]{1,3,2,0:T(8,128)} %bitcast.148, f32[512]{0:T(512)S(1)} %get-tuple-element.100, f32[512]{0:T(512)S(1)} %get-tuple-element.101, f32[512]{0:T(512)S(1)} %get-tuple-element.102, ...), kind=kLoop, calls=%fused_computation.95 | loop fusion | flops 3407872 | bytes 5257216 | tf_op jit(solution)/shard_map/sub | solution.py:81
  103.0 1.4 copy.146
  104.4 2.6 %copy.148 = f32[1,512,4,128]{3,2,1,0:T(4,128)} copy(f32[1,512,4,128]{1,3,2,0:T(8,128)} %get-tuple-element.48) | data formatting | bytes 2097152 | tf_op jit(solution)/shard_map/sub | solution.py:81
  107.1 2.8 %pad_maximum_fusion.5 = f32[2,512,4,128]{1,3,2,0:T(8,128)} fusion(f32[1,512,4,128]{1,3,2,0:T(8,128)} %get-tuple-element.48, f32[1,512,4,128]{1,3,2,0:T(8,128)S(1)} %get-tuple-element.47), kind=kLoop, calls=%fused_computation.39 | loop fusion | flops 524288 | bytes 4194304 | tf_op jit(solution)/shard_map/stack | solution.py:81
  109.8 2.9 %copy.149 = f32[2,512,4,128]{3,2,1,0:T(4,128)} copy(f32[2,512,4,128]{1,3,2,0:T(8,128)} %pad_maximum_fusion.5) | data formatting | bytes 4194304 | tf_op jit(solution)/shard_map/stack | solution.py:81
  112.8 5.3 %multiply_reduce_fusion = f32[4,2]{1,0:T(4,128)S(1)} fusion(bf16[4,2,512,4,128]{4,3,2,1,0:T(4,128)(2,1)} %param.13, f32[2,512,4,128]{3,2,1,0:T(4,128)} %copy.149), kind=kLoop, calls=%fused_computation | loop fusion | flops 6291448 | bytes 6291488 | tf_op jit(solution)/shard_map/reduce_sum | solution.py:83
  118.1 2.3 %fusion.15 = f32[2]{0:T(128)S(1)} fusion(f32[1,262144]{1,0:T(1,128)S(1)} %bitcast.146, f32[1,262144]{1,0:T(1,128)S(1)} %bitcast.145), kind=kLoop, calls=%fused_computation.38 | loop fusion | flops 1572862 | bytes 2097160 | tf_op jit(solution)/shard_map/reduce_sum | solution.py:84
  120.4 40.7 %all-reduce.1 = (f32[2,4,4]{2,1,0:T(4,128)S(1)}, f32[2,4]{0,1:T(4,128)S(1)}, f32[2]{0:T(128)S(1)}) all-reduce(f32[2,4,4]{2,1,0:T(4,128)S(1)} %fusion, f32[2,4]{0,1:T(4,128)S(1)} %bitcast.156, f32[2]{0:T(128)S(1)} %fusion.15), channel_id=1, replica_groups=mesh['egrp'=2,'space'=16] {'egrp','space'}, use_global_device_ids=true, to_apply=%region_4.5 | all-reduce | flops 42 | bytes 336 | tf_op jit(solution)/shard_map/psum | solution.py:88
  161.3 0.6 fusion.88
  162.0 0.7 maximum_bitcast_fusion.1
  163.7 0.7 compare_reduce_fusion
  164.4 0.6 fusion.50
  165.6 0.8 fusion.93
  166.4 0.6 broadcast_divide_fusion
  167.0 0.7 fusion.89
  167.7 0.7 maximum_bitcast_fusion
  169.4 0.6 compare_reduce_fusion.1
  170.0 0.6 fusion.49
  171.3 0.8 fusion.92
  172.0 0.6 broadcast_divide_fusion.1
  172.7 0.7 fusion.87
  173.4 6.4 %bitcast_add_fusion = f32[1,512,4,128]{1,3,2,0:T(8,128)S(1)} fusion(bf16[1,1,512,4,128]{2,4,3,1,0:T(8,128)(2,1)} %copy.198, bf16[1,1,512,4,128]{2,4,3,1,0:T(8,128)(2,1)} %copy.197, bf16[1,1,512,4,128]{2,4,3,1,0:T(8,128)(2,1)} %copy.196, bf16[1,1,512,4,128]{2,4,3,1,0:T(8,128)(2,1)} %copy.195, bf16[1,1,512,4,128]{2,4,3,1,0:T(8,128)(2,1)} %copy.194, ...), kind=kLoop, calls=%fused_computation.87 | loop fusion | flops 9175040 | bytes 6303764 | tf_op jit(solution)/shard_map/add | solution.py:101
  179.9 4.2 %bitcast_add_fusion.4 = f32[1,512,4,128]{1,3,2,0:T(8,128)S(1)} fusion(bf16[1,1,512,4,128]{2,4,3,1,0:T(8,128)(2,1)S(1)} %copy-done.9, bf16[1,1,512,4,128]{2,4,3,1,0:T(8,128)(2,1)S(1)} %copy-done.8, bf16[1,1,512,4,128]{2,4,3,1,0:T(8,128)(2,1)S(1)} %copy-done.7, bf16[1,1,512,4,128]{2,4,3,1,0:T(8,128)(2,1)S(1)} %copy-done.6, ...), kind=kLoop, calls=%fused_computation.91 | loop fusion | flops 7077888 | bytes 7340052 | tf_op jit(solution)/shard_map/add | solution.py:101
  184.2 4.5 %collective-permute-start.1 = (f32[2,512,1,128]{1,3,2,0:T(8,128)S(1)}, f32[2,512,1,128]{1,3,2,0:T(8,128)S(1)}, u32[]{:S(2)}, u32[]{:S(2)}) collective-permute-start(f32[2,512,1,128]{1,3,2,0:T(8,128)S(1)} %get-tuple-element.41), channel_id=1, source_target_pairs={{0,1},{1,2},{2,3},{3,4},{4,5},{5,6},{6,7},{7,8},{8,9},{9,10},{10,1... | collective-permute-start | bytes 1572872 | tf_op jit(solution)/shard_map/ppermute | solution.py:26
  188.7 1.9 collective-permute-start.3
  191.4 9.0 %collective-permute-done.1 = f32[2,512,1,128]{1,3,2,0:T(8,128)S(1)} collective-permute-done((f32[2,512,1,128]{1,3,2,0:T(8,128)S(1)}, f32[2,512,1,128]{1,3,2,0:T(8,128)S(1)}, u32[]{:S(2)}, u32[]{:S(2)}) %collective-permute-start.1) | collective-permute-done | bytes 524320 | tf_op jit(solution)/shard_map/ppermute | solution.py:26
  200.4 1.6 collective-permute-done.3
  202.0 2.9 %fusion.11 = f32[2,512,4,128]{1,3,2,0:T(8,128)S(1)} fusion(f32[2,512,1,128]{1,3,2,0:T(8,128)S(1)} %collective-permute-done.3, f32[1,512,4,128]{1,3,2,0:T(8,128)S(1)} %bitcast_add_fusion, f32[1,512,4,128]{1,3,2,0:T(8,128)S(1)} %bitcast_add_fusion.4, f32[2,512,1,128]{1,3,2,0:T(8,128)S(1)} %collective-permute-done.1, ...), kind=kLoop, calls=%fused_computation.30 | loop fusion | flops 15204352 | bytes 11545096 | tf_op jit(solution)/shard_map/add | solution.py:35
  204.9 0.5 fusion.44
  205.6 1.8 copy.178
  (78 shorter events, 5.7 us)
Async XLA Ops:
  3.5 4.9 %copy-start.10 = (f32[4,128]{1,0:T(4,128)S(1)}, f32[4,128]{1,0:T(4,128)}, u32[]{:S(2)}) copy-start(f32[4,128]{1,0:T(4,128)} %param.14) | copy-start | bytes 6148
  3.5 10.8 %copy-start.11 = (s32[4]{0:T(128)S(1)}, s32[4]{0:T(128)}, u32[]{:S(2)}) copy-start(s32[4]{0:T(128)} %param.16) | copy-start | bytes 52
  4.6 68.0 %all-to-all-start = ((f32[2,512,256]{2,1,0:T(8,128)}), f32[2,512,256]{2,1,0:T(8,128)S(1)}, u32[]{:S(2)}, u32[]{:S(2)}) async-start(f32[2,512,256]{2,1,0:T(8,128)} %pad_maximum_fusion.7), calls=%async_computation | async-start | bytes 2097152 | tf_op jit(solution)/shard_map/all_to_all | solution.py:16
  8.4 90.3 %collective-permute-start = (f32[1,1,1,128]{3,2,1,0:T(1,128)S(1)}, f32[1,1,1,128]{3,2,1,0:T(1,128)S(1)}, u32[]{:S(2)}, u32[]{:S(2)}) collective-permute-start(f32[1,1,1,128]{3,2,1,0:T(1,128)S(1)} %get-tuple-element.55), channel_id=1, source_target_pairs={{0,1},{1,2},{2,3},{3,4},{4,5},{5,6},{6,7},{7,8},{8,9},{9,10},{10,1... | collective-permute-start | bytes 1544 | tf_op jit(solution)/shard_map/ppermute | solution.py:26
  12.4 86.4 %collective-permute-start.2 = (f32[1,1,1,128]{3,2,1,0:T(1,128)S(1)}, f32[1,1,1,128]{3,2,1,0:T(1,128)S(1)}, u32[]{:S(2)}, u32[]{:S(2)}) collective-permute-start(f32[1,1,1,128]{3,2,1,0:T(1,128)S(1)} %get-tuple-element.56), channel_id=1, source_target_pairs={{1,0},{2,1},{3,2},{4,3},{5,4},{6,5},{7,6},{8,7},{9,8},{10,9},{11,1... | collective-permute-start | bytes 1544 | tf_op jit(solution)/shard_map/ppermute | solution.py:29
  30.6 4.4 %copy-start.12 = (f32[4]{0:T(128)S(1)}, f32[4]{0:T(128)}, u32[]{:S(2)}) copy-start(f32[4]{0:T(128)} %param.17) | copy-start | bytes 52
  30.6 10.2 %copy-start.13 = (s32[4,128]{1,0:T(4,128)S(1)}, s32[4,128]{1,0:T(4,128)}, u32[]{:S(2)}) copy-start(s32[4,128]{1,0:T(4,128)} %param.15) | copy-start | bytes 6148
  34.8 10.1 %copy-start.14 = (s32[2,4]{1,0:T(2,128)S(1)}, s32[2,4]{1,0:T(2,128)}, u32[]{:S(2)}) copy-start(s32[2,4]{1,0:T(2,128)} %param.18) | copy-start | bytes 100
  74.8 23.9 %all-to-all-start.1 = ((f32[2,512,256]{2,1,0:T(8,128)}), f32[2,512,256]{2,1,0:T(8,128)S(1)}, u32[]{:S(2)}, u32[]{:S(2)}) async-start(f32[2,512,256]{2,1,0:T(8,128)} %bitcast.144), calls=%async_computation.1 | async-start | bytes 2097152 | tf_op jit(solution)/shard_map/all_to_all | solution.py:75
  112.8 5.3 %copy-start = (f32[1,512,4,128]{3,2,1,0:T(4,128)S(1)}, f32[1,512,4,128]{3,2,1,0:T(4,128)}, u32[]{:S(2)}) copy-start(f32[1,512,4,128]{3,2,1,0:T(4,128)} %copy.146) | copy-start | bytes 3145732
  112.8 5.3 %copy-start.1 = (f32[1,512,4,128]{3,2,1,0:T(4,128)S(1)}, f32[1,512,4,128]{3,2,1,0:T(4,128)}, u32[]{:S(2)}) copy-start(f32[1,512,4,128]{3,2,1,0:T(4,128)} %copy.148) | copy-start | bytes 3145732
  173.4 6.5 %copy-start.2 = (bf16[1,1,512,4,128]{2,4,3,1,0:T(8,128)(2,1)S(1)}, bf16[1,1,512,4,128]{2,4,3,1,0:T(8,128)(2,1)}, u32[]{:S(2)}) copy-start(bf16[1,1,512,4,128]{2,4,3,1,0:T(8,128)(2,1)} %copy.183) | copy-start | bytes 1572868
  173.4 6.5 %copy-start.3 = (bf16[1,1,512,4,128]{2,4,3,1,0:T(8,128)(2,1)S(1)}, bf16[1,1,512,4,128]{2,4,3,1,0:T(8,128)(2,1)}, u32[]{:S(2)}) copy-start(bf16[1,1,512,4,128]{2,4,3,1,0:T(8,128)(2,1)} %copy.184) | copy-start | bytes 1572868
  173.4 6.5 %copy-start.4 = (bf16[1,1,512,4,128]{2,4,3,1,0:T(8,128)(2,1)S(1)}, bf16[1,1,512,4,128]{2,4,3,1,0:T(8,128)(2,1)}, u32[]{:S(2)}) copy-start(bf16[1,1,512,4,128]{2,4,3,1,0:T(8,128)(2,1)} %copy.185) | copy-start | bytes 1572868
  173.4 6.5 %copy-start.5 = (bf16[1,1,512,4,128]{2,4,3,1,0:T(8,128)(2,1)S(1)}, bf16[1,1,512,4,128]{2,4,3,1,0:T(8,128)(2,1)}, u32[]{:S(2)}) copy-start(bf16[1,1,512,4,128]{2,4,3,1,0:T(8,128)(2,1)} %copy.186) | copy-start | bytes 1572868
  173.4 6.5 %copy-start.6 = (bf16[1,1,512,4,128]{2,4,3,1,0:T(8,128)(2,1)S(1)}, bf16[1,1,512,4,128]{2,4,3,1,0:T(8,128)(2,1)}, u32[]{:S(2)}) copy-start(bf16[1,1,512,4,128]{2,4,3,1,0:T(8,128)(2,1)} %copy.187) | copy-start | bytes 1572868
  173.4 6.5 %copy-start.7 = (bf16[1,1,512,4,128]{2,4,3,1,0:T(8,128)(2,1)S(1)}, bf16[1,1,512,4,128]{2,4,3,1,0:T(8,128)(2,1)}, u32[]{:S(2)}) copy-start(bf16[1,1,512,4,128]{2,4,3,1,0:T(8,128)(2,1)} %copy.188) | copy-start | bytes 1572868
  173.4 6.5 %copy-start.8 = (bf16[1,1,512,4,128]{2,4,3,1,0:T(8,128)(2,1)S(1)}, bf16[1,1,512,4,128]{2,4,3,1,0:T(8,128)(2,1)}, u32[]{:S(2)}) copy-start(bf16[1,1,512,4,128]{2,4,3,1,0:T(8,128)(2,1)} %copy.189) | copy-start | bytes 1572868
  173.4 6.5 %copy-start.9 = (bf16[1,1,512,4,128]{2,4,3,1,0:T(8,128)(2,1)S(1)}, bf16[1,1,512,4,128]{2,4,3,1,0:T(8,128)(2,1)}, u32[]{:S(2)}) copy-start(bf16[1,1,512,4,128]{2,4,3,1,0:T(8,128)(2,1)} %copy.190) | copy-start | bytes 1572868
  184.2 16.2 %collective-permute-start.1 = (f32[2,512,1,128]{1,3,2,0:T(8,128)S(1)}, f32[2,512,1,128]{1,3,2,0:T(8,128)S(1)}, u32[]{:S(2)}, u32[]{:S(2)}) collective-permute-start(f32[2,512,1,128]{1,3,2,0:T(8,128)S(1)} %get-tuple-element.41), channel_id=1, source_target_pairs={{0,1},{1,2},{2,3},{3,4},{4,5},{5,6},{6,7},{7,8},{8,9},{9,10},{10,1... | collective-permute-start | bytes 1572872 | tf_op jit(solution)/shard_map/ppermute | solution.py:26
  188.7 13.3 %collective-permute-start.3 = (f32[2,512,1,128]{1,3,2,0:T(8,128)S(1)}, f32[2,512,1,128]{1,3,2,0:T(8,128)S(1)}, u32[]{:S(2)}, u32[]{:S(2)}) collective-permute-start(f32[2,512,1,128]{1,3,2,0:T(8,128)S(1)} %get-tuple-element.42), channel_id=1, source_target_pairs={{1,0},{2,1},{3,2},{4,3},{5,4},{6,5},{7,6},{8,7},{9,8},{10,9},{11,1... | collective-permute-start | bytes 1572872 | tf_op jit(solution)/shard_map/ppermute | solution.py:29
